TPU v7x, 32 devices: a whole 2x2x4 slice. The times are simulated.
32 devices in a mesh: query: 8 (over y, x, core), tok: 4 (over z).
Axes of the slice: x: 2, y: 2, z: 4, core: 2. Of those that a mesh axis runs over, the one named last changes fastest.
Arguments:
- query_acts: bfloat16 [8, 1024, 4096], P('query', 'tok'), may hold values from -6 to 6
- query_grads: bfloat16 [8, 1024, 512], P('query', 'tok'), may hold values from -6 to 6
- sketch_maps: bfloat16 [8, 32, 512], P('query'), may hold values from -0.25 to 0.25
- res_acts: bfloat16 [32768, 4096], P(('query', 'tok')), may hold values from -6 to 6
- res_grads: bfloat16 [32768, 512], P(('query', 'tok')), may hold values from -6 to 6
Outputs:
- scores: float32 [8, 32768], P(None, ('query', 'tok'))
All inputs are finite; a program needn't handle non-finite values.
Results may differ from a plain program's by a relative error of at most 0.0054.
Values may be sent and summed in bfloat16 or wider, within the bound.
A program may use at most 64 MiB of HBM per device.

v0:
```python
import functools
import math

import jax
import jax.numpy as jnp
from jax import lax
from jax.experimental import pallas as pl
from jax.experimental.pallas import tpu as pltpu
from jax.sharding import PartitionSpec as P

MESH = pl.DeviceIdType.MESH
F32 = jnp.float32
BF16 = jnp.bfloat16


def contract_last(first_arr, second_arr):
    return lax.dot_general(first_arr, second_arr, (((1,), (1,)), ((), ())), preferred_element_type=F32)


def spd_inverse(gram):
    size = gram.shape[0]
    rows = lax.broadcasted_iota(jnp.int32, (size, 2 * size), 0)
    cols = lax.broadcasted_iota(jnp.int32, (size, size), 1)
    eye = jnp.where(rows[:, :size] == cols, 1.0, 0.0).astype(F32)
    aug = jnp.concatenate([gram, eye], axis=1)
    for k in range(size):
        row = aug[k : k + 1, :] / aug[k : k + 1, k : k + 1]
        aug = jnp.where(rows == k, row, aug - aug[:, k : k + 1] * row)
    return aug[:, size:]


def kernel(
    n_q, n_t, scale,
    a_hbm, g_hbm, m_hbm, ra_hbm, rg_hbm, out_ref,
    a_buf, g_buf, m_buf, ra_buf, rg_buf,
    part_buf, rs_buf, s_all, r_mine, r_recv, x_all, acc,
    local_sem, rs_s, rs_r, z_s, z_r, c_s, c_r, b_s, b_r, f_s, f_r, x_s, x_r,
):
    q, z = lax.axis_index("query"), lax.axis_index("tok")
    n_chip = n_q // 2
    chip, core = q // 2, lax.rem(q, 2)
    sibling = chip * 2 + 1 - core
    rank = m_buf.shape[0]
    width = a_buf.shape[2]

    def tok_at(i):
        return lax.rem(z + i + n_t, n_t)

    def chip_at(c, which):
        return lax.rem(chip + c + n_chip, n_chip) * 2 + which

    loads = []

    def load(src, dst):
        copy = pltpu.make_async_copy(src, dst, local_sem.at[len(loads)])
        copy.start()
        loads.append(copy)
        return copy

    load_m = load(m_hbm, m_buf)
    load_g = load(g_hbm, g_buf)
    load_a, load_ra = [], []
    for i in range(n_t):
        t = tok_at(i + 1)
        load_a.append(load(a_hbm.at[:, pl.ds(pl.multiple_of(t * width, width), width)], a_buf.at[t]))
    barrier = pltpu.get_barrier_semaphore()
    for i in range(1, n_t):
        pl.semaphore_signal(barrier, inc=1, device_id=(q, tok_at(i)), device_id_type=MESH)
    for i in range(1, n_q):
        pl.semaphore_signal(barrier, inc=1, device_id=(lax.rem(q + i, n_q), z), device_id_type=MESH)

    sent = []

    def send(src, dst, send_sem, recv_sem, device):
        copy = pltpu.make_async_remote_copy(
            src_ref=src, dst_ref=dst, send_sem=send_sem, recv_sem=recv_sem, device_id=device, device_id_type=MESH
        )
        copy.start()
        sent.append(copy)

    def landed(dst, send_sem, recv_sem, device):
        pltpu.make_async_remote_copy(
            src_ref=dst, dst_ref=dst, send_sem=send_sem, recv_sem=recv_sem, device_id=device, device_id_type=MESH
        ).wait_recv()

    load_m.wait()
    load_g.wait()
    projected = contract_last(m_buf[...], g_buf[...]).astype(BF16)
    chunk = None
    for i in range(1, n_t + 1):
        t = tok_at(i)
        load_a[i - 1].wait()
        part = jnp.dot(projected, a_buf[t], preferred_element_type=F32)
        if i == n_t:
            chunk = part
        else:
            part_buf[i - 1] = part.astype(BF16)
    for i in range(n_t):
        t = tok_at(-i)
        load_ra.append(load(ra_hbm.at[:, pl.ds(pl.multiple_of(t * width, width), width)], ra_buf.at[t]))
    load_rg = load(rg_hbm, rg_buf)
    pl.semaphore_wait(barrier, n_t - 1 + n_q - 1)
    for i in range(1, n_t):
        send(part_buf.at[i - 1], rs_buf.at[i - 1], rs_s.at[i - 1], rs_r.at[i - 1], (q, tok_at(i)))
    for i in range(1, n_t):
        landed(rs_buf.at[i - 1], rs_s.at[i - 1], rs_r.at[i - 1], (q, tok_at(-i)))
        chunk = chunk + rs_buf[i - 1].astype(F32)

    def block(t, owner):
        return s_all.at[t, pl.ds(pl.multiple_of(owner * rank, rank), rank), :]

    s_all[z, pl.ds(pl.multiple_of(q * rank, rank), rank), :] = chunk.astype(BF16)

    def spread(i):
        here = block(tok_at(-i), q)
        for c in range(1, n_chip):
            send(here, here, c_s.at[c - 1, i], c_r.at[c - 1, i], (chip_at(c, core), z))
        send(here, here, b_s.at[0, i], b_r.at[0, i], (sibling, z))

    for i in range(1, n_t):
        send(block(z, q), block(z, q), z_s.at[i - 1], z_r.at[i - 1], (q, tok_at(i)))
    gram = jnp.zeros((rank, rank), F32)
    pulled = jnp.zeros((rank, g_buf.shape[0]), F32)
    for i in range(n_t):
        t = tok_at(-i)
        if i:
            landed(block(t, q), z_s.at[i - 1], z_r.at[i - 1], (q, t))
        spread(i)
        mine = s_all[t, pl.ds(pl.multiple_of(q * rank, rank), rank), :]
        pulled += contract_last(mine, a_buf[t])
        gram += contract_last(mine, mine)
    high = pulled.astype(BF16)
    low = (pulled - high.astype(F32)).astype(BF16)
    grads = g_buf[...]
    right = jnp.dot(high, grads, preferred_element_type=F32) + jnp.dot(low, grads, preferred_element_type=F32)
    r_mine[...] = right.astype(BF16)
    for i in range(1, n_t):
        send(r_mine, r_recv.at[i - 1], f_s.at[i - 1], f_r.at[i - 1], (q, tok_at(i)))

    def relay(i):
        t = tok_at(-i)
        for c in range(1, n_chip):
            owner = chip_at(-c, core)
            landed(block(t, owner), c_s.at[c - 1, i], c_r.at[c - 1, i], (owner, z))
            send(block(t, owner), block(t, owner), b_s.at[c, i], b_r.at[c, i], (sibling, z))

    def score(i):
        t = tok_at(-i)
        for c in range(n_chip):
            landed(block(t, chip_at(-c, 1 - core)), b_s.at[c, i], b_r.at[c, i], (sibling, z))
        load_ra[i].wait()
        term = contract_last(s_all[t], ra_buf[t])
        if i == 0:
            acc[...] = term
        else:
            acc[...] += term


    def x_block(owner):
        return x_all.at[pl.ds(pl.multiple_of(owner * rank, rank), rank), :]

    def solve(inverse, right):
        for i in range(1, n_t):
            landed(r_recv.at[i - 1], f_s.at[i - 1], f_r.at[i - 1], (q, tok_at(-i)))
            right = right + r_recv[i - 1].astype(F32)
        solved = jnp.dot(inverse, right, precision=lax.Precision.HIGHEST, preferred_element_type=F32)
        x_all[pl.ds(pl.multiple_of(q * rank, rank), rank), :] = solved.astype(BF16)
        for i in (*range(2, n_q), 1):
            send(x_block(q), x_block(q), x_s.at[i - 1], x_r.at[i - 1], (lax.rem(q + i, n_q), z))

    relay(0)
    inverse = spd_inverse(gram)
    relay(1)
    solve(inverse, right)
    score(0)
    for i in range(2, n_t):
        relay(i)
        score(i - 1)
    score(n_t - 1)
    load_rg.wait()
    for i in range(1, n_q):
        owner = lax.rem(q + n_q - i, n_q)
        landed(x_block(owner), x_s.at[i - 1], x_r.at[i - 1], (owner, z))
    product = contract_last(x_all[...], rg_buf[...]) * acc[...]
    totals = jnp.sum(product.reshape(n_q, rank, product.shape[1]), axis=1)
    out_ref[...] = totals * scale
    for copy in sent:
        copy.wait_send()


def local(query_acts, query_grads, sketch_maps, res_acts, res_grads):
    n_q, n_t = lax.axis_size("query"), lax.axis_size("tok")
    _, tokens, d_in = query_acts.shape
    d_out = query_grads.shape[2]
    rank = sketch_maps.shape[1]
    resident = res_acts.shape[0]
    width = d_in // n_t
    scale = 1.0 / math.sqrt(rank * d_out * tokens * n_t)
    n_chip = n_q // 2
    dma = pltpu.SemaphoreType.DMA
    vmem = pltpu.VMEM
    any_spec = pl.BlockSpec(memory_space=pl.ANY)
    return pl.pallas_call(
        functools.partial(kernel, n_q, n_t, scale),
        out_shape=jax.ShapeDtypeStruct((n_q, resident), F32),
        in_specs=[any_spec] * 5,
        out_specs=pl.BlockSpec(memory_space=pltpu.VMEM),
        scratch_shapes=[
            vmem((n_t, tokens, width), BF16),
            vmem((tokens, d_out), BF16),
            vmem((rank, d_out), BF16),
            vmem((n_t, resident, width), BF16),
            vmem((resident, d_out), BF16),
            vmem((n_t - 1, rank, width), BF16),
            vmem((n_t - 1, rank, width), BF16),
            vmem((n_t, n_q * rank, width), BF16),
            vmem((rank, d_out), BF16),
            vmem((n_t - 1, rank, d_out), BF16),
            vmem((n_q * rank, d_out), BF16),
            vmem((n_q * rank, resident), F32),
            dma((2 * n_t + 3,)),
            dma((n_t - 1,)), dma((n_t - 1,)),
            dma((n_t - 1,)), dma((n_t - 1,)),
            dma((n_chip - 1, n_t)), dma((n_chip - 1, n_t)),
            dma((n_chip, n_t)), dma((n_chip, n_t)),
            dma((n_t - 1,)), dma((n_t - 1,)),
            dma((n_q - 1,)), dma((n_q - 1,)),
        ],
        compiler_params=pltpu.CompilerParams(
            collective_id=0, has_side_effects=True, vmem_limit_bytes=60 * 1024 * 1024
        ),
    )(query_acts[0], query_grads[0], sketch_maps[0], res_acts, res_grads)


def solution(mesh):
    in_specs = (
        P("query", "tok", None),
        P("query", "tok", None),
        P("query", None, None),
        P(("query", "tok"), None),
        P(("query", "tok"), None),
    )
    out_specs = P(None, ("query", "tok"))
    return jax.shard_map(local, mesh=mesh, in_specs=in_specs, out_specs=out_specs, check_vma=False)
```

profile of v0, /device:TPU:0, one launch (start us, length us, event | category | flops | bytes accessed | tf_op | source)
XLA Modules:
  0.0 31.5 jit_solution(13529963482572926119)
XLA Ops:
  0.0 30.2 %shard_map.55 = f32[8,1024]{1,0:T(8,128)} custom-call(bf16[256,4096]{1,0:T(8,128)(2,1)} %bitcast.3, bf16[256,512]{1,0:T(8,128)(2,1)} %bitcast.4, bf16[32,512]{1,0:T(8,128)(2,1)} %bitcast.5, bf16[1024,4096]{1,0:T(8,128)(2,1)} %ra_hbm.1, bf16[1024,512]{1,0:T(8,128)(2,1)} %rg_hbm.1), custom_call_target="tpu_custom_call" | custom-call | tf_op jit(solution)/shard_map/pallas_call | solution.py:203
  30.2 1.4 %copy.7 = f32[8,1024]{1,0:T(8,128)} copy(f32[8,1024]{1,0:T(8,128)} %shard_map.55) | data formatting | bytes 65536
where the time goes:
time: 31.7 us; the launch traced here: 31.5 us
  Pallas kernels  30.2 us (95%)
  local copies, waits for them, and re-layouts  1.38 us (4%)
    pallas_call x1, Pallas kernels, local(): pl.pallas_call(functools.partial(kernel, n_q, n_t, scale), out_shape=jax....  30.2 us
    unnamed x1, local copies, waits for them, and re-layouts  1.38 us

commit v1 on v0

--- a/solution.py
+++ b/solution.py
@@ -202,7 +202,7 @@
     any_spec = pl.BlockSpec(memory_space=pl.ANY)
     return pl.pallas_call(
         functools.partial(kernel, n_q, n_t, scale),
-        out_shape=jax.ShapeDtypeStruct((n_q, resident), F32),
+        out_shape=pltpu.VMEM((n_q, resident), F32),
         in_specs=[any_spec] * 5,
         out_specs=pl.BlockSpec(memory_space=pltpu.VMEM),
         scratch_shapes=[

time: 31.7 us -> 30.3 us (0.956)
  local copies, waits for them, and re-layouts: 1.38 us -> 0.62 us
  Pallas kernels: 30.2 us -> 29.6 us
    unnamed x1, local copies, waits for them, and re-layouts: 1.38 us -> 0.62 us
    pallas_call x1, Pallas kernels: 30.2 us -> 29.6 us  [local(): pl.pallas_call(functools.partial(kernel, n_q, n_t, scale), out_shape=pltp...]
where the time goes in v1:
time: 30.3 us; the launch traced here: 30.2 us
  Pallas kernels  29.6 us (98%)
  local copies, waits for them, and re-layouts  0.62 us (2%)
    pallas_call x1, Pallas kernels, local(): pl.pallas_call(functools.partial(kernel, n_q, n_t, scale), out_shape=pltp...  29.6 us
    unnamed x1, local copies, waits for them, and re-layouts  0.62 us

profile of v1, /device:TPU:0, one launch (start us, length us, event | category | flops | bytes accessed | tf_op | source)
XLA Modules:
  0.0 30.2 jit_solution(11156774953094006369)
XLA Ops:
  0.0 29.6 %shard_map.55 = f32[8,1024]{1,0:T(8,128)S(1)} custom-call(bf16[256,4096]{1,0:T(8,128)(2,1)} %bitcast.3, bf16[256,512]{1,0:T(8,128)(2,1)} %bitcast.4, bf16[32,512]{1,0:T(8,128)(2,1)} %bitcast.5, bf16[1024,4096]{1,0:T(8,128)(2,1)} %ra_hbm.1, bf16[1024,512]{1,0:T(8,128)(2,1)} %rg_hbm.1), custom_call_target="tpu_custom_call" | custom-call | tf_op jit(solution)/shard_map/pallas_call | solution.py:203
  29.6 0.6 %copy.7 = f32[8,1024]{1,0:T(8,128)} copy(f32[8,1024]{1,0:T(8,128)S(1)} %shard_map.55) | data formatting | bytes 65536

commit v2 on v1

v2 whole, which is shorter than its diff:
```python
import functools
import math

import jax
import jax.numpy as jnp
from jax import lax
from jax.experimental import pallas as pl
from jax.experimental.pallas import tpu as pltpu
from jax.sharding import PartitionSpec as P

MESH = pl.DeviceIdType.MESH
F32 = jnp.float32
BF16 = jnp.bfloat16


def contract_last(first_arr, second_arr):
    return lax.dot_general(first_arr, second_arr, (((1,), (1,)), ((), ())), preferred_element_type=F32)


def spd_inverse(gram):
    size = gram.shape[0]
    rows = lax.broadcasted_iota(jnp.int32, (size, 2 * size), 0)
    cols = lax.broadcasted_iota(jnp.int32, (size, size), 1)
    eye = jnp.where(rows[:, :size] == cols, 1.0, 0.0).astype(F32)
    aug = jnp.concatenate([gram, eye], axis=1)
    for k in range(size):
        row = aug[k : k + 1, :] / aug[k : k + 1, k : k + 1]
        aug = jnp.where(rows == k, row, aug - aug[:, k : k + 1] * row)
    return aug[:, size:]


def kernel(
    n_q, n_t, scale,
    a_hbm, g_hbm, m_hbm, ra_hbm, rg_hbm, out_ref,
    a_buf, g_buf, m_buf, ra_buf, rg_buf,
    part_buf, rs_buf, s_all, r_mine, r_recv, x_all, acc,
    local_sem, rs_s, rs_r, z_s, z_r, s_s, c_r, b_r, f_s, f_r, x_s, x_r,
):
    q, z = lax.axis_index("query"), lax.axis_index("tok")
    n_chip = n_q // 2
    chip, core = q // 2, lax.rem(q, 2)
    sibling = chip * 2 + 1 - core
    rank = m_buf.shape[0]
    width = a_buf.shape[2]

    def tok_at(i):
        return lax.rem(z + i + n_t, n_t)

    def chip_at(c, which):
        return lax.rem(chip + c + n_chip, n_chip) * 2 + which

    def load(src, dst, sem):
        copy = pltpu.make_async_copy(src, dst, local_sem.at[sem])
        copy.start()
        return copy

    load_m = load(m_hbm, m_buf, 0)
    load_g = load(g_hbm, g_buf, 1)
    load_a, load_ra = [], []
    for i in range(n_t):
        t = tok_at(i + 1)
        load_a.append(load(a_hbm.at[:, pl.ds(pl.multiple_of(t * width, width), width)], a_buf.at[t], 2 + i))
    barrier = pltpu.get_barrier_semaphore()
    for i in range(1, n_t):
        pl.semaphore_signal(barrier, inc=1, device_id=(q, tok_at(i)), device_id_type=MESH)
    for i in range(1, n_q):
        pl.semaphore_signal(barrier, inc=1, device_id=(lax.rem(q + i, n_q), z), device_id_type=MESH)

    def remote(src, dst, send_sem, recv_sem, device):
        return pltpu.make_async_remote_copy(
            src_ref=src, dst_ref=dst, send_sem=send_sem, recv_sem=recv_sem, device_id=device, device_id_type=MESH
        )

    def send(src, dst, send_sem, recv_sem, device):
        remote(src, dst, send_sem, recv_sem, device).start()

    def landed(like, sem):
        remote(like, like, sem, sem, (sibling, z)).wait_recv()

    def left(like, sem):
        remote(like, like, sem, sem, (sibling, z)).wait_send()

    load_m.wait()
    load_g.wait()
    projected = contract_last(m_buf[...], g_buf[...]).astype(BF16)
    chunk = None
    for i in range(1, n_t + 1):
        t = tok_at(i)
        load_a[i - 1].wait()
        part = jnp.dot(projected, a_buf[t], preferred_element_type=F32)
        if i == n_t:
            chunk = part
        else:
            part_buf[i - 1] = part.astype(BF16)
    for i in range(n_t):
        t = tok_at(-i)
        load_ra.append(load(ra_hbm.at[:, pl.ds(pl.multiple_of(t * width, width), width)], ra_buf.at[t], 2 + i))
    load_rg = load(rg_hbm, rg_buf, 0)
    pl.semaphore_wait(barrier, n_t - 1 + n_q - 1)
    for i in range(1, n_t):
        send(part_buf.at[i - 1], rs_buf.at[i - 1], rs_s, rs_r.at[i - 1], (q, tok_at(i)))
    for i in range(1, n_t):
        landed(rs_buf.at[i - 1], rs_r.at[i - 1])
        chunk = chunk + rs_buf[i - 1].astype(F32)

    def block(t, owner):
        return s_all.at[t, pl.ds(pl.multiple_of(owner * rank, rank), rank), :]

    s_all[z, pl.ds(pl.multiple_of(q * rank, rank), rank), :] = chunk.astype(BF16)

    def from_chip(c, i):
        return c_r.at[c - 1, i]

    def spread(i):
        here = block(tok_at(-i), q)
        for c in range(1, n_chip):
            send(here, here, s_s, from_chip(c, i), (chip_at(c, core), z))
        send(here, here, s_s, b_r.at[i], (sibling, z))

    for i in range(1, n_t):
        send(block(z, q), block(z, q), z_s, z_r.at[i - 1], (q, tok_at(i)))
    gram = jnp.zeros((rank, rank), F32)
    pulled = jnp.zeros((rank, g_buf.shape[0]), F32)
    for i in range(n_t):
        t = tok_at(-i)
        if i:
            landed(block(t, q), z_r.at[i - 1])
        spread(i)
        mine = s_all[t, pl.ds(pl.multiple_of(q * rank, rank), rank), :]
        pulled += contract_last(mine, a_buf[t])
        if i < n_t - 1:
            gram += contract_last(mine, mine)
    high = pulled.astype(BF16)
    low = (pulled - high.astype(F32)).astype(BF16)
    grads = g_buf[...]
    right = jnp.dot(high, grads, preferred_element_type=F32) + jnp.dot(low, grads, preferred_element_type=F32)
    r_mine[...] = right.astype(BF16)
    for i in range(1, n_t):
        send(r_mine, r_recv.at[i - 1], f_s, f_r, (q, tok_at(i)))
    gram += contract_last(mine, mine)

    def relay(i):
        t = tok_at(-i)
        for c in range(1, n_chip):
            here = block(t, chip_at(-c, core))
            landed(here, from_chip(c, i))
            send(here, here, s_s, b_r.at[i], (sibling, z))

    def ready(i):
        landed(s_all.at[tok_at(-i), pl.ds(0, n_chip * rank)], b_r.at[i])
        load_ra[i].wait()

    def term(i):
        t = tok_at(-i)
        return contract_last(s_all[t], ra_buf[t])

    def score(i):
        ready(i)
        if i == 0:
            acc[...] = term(i)
        else:
            acc[...] += term(i)

    def x_block(owner):
        return x_all.at[pl.ds(pl.multiple_of(owner * rank, rank), rank), :]

    def solve(inverse, right):
        landed(r_recv, f_r)
        for i in range(1, n_t):
            right = right + r_recv[i - 1].astype(F32)
        solved = jnp.dot(inverse, right, precision=lax.Precision.HIGHEST, preferred_element_type=F32)
        x_all[pl.ds(pl.multiple_of(q * rank, rank), rank), :] = solved.astype(BF16)
        for i in (*range(2, n_q), 1):
            send(x_block(q), x_block(q), x_s, x_r, (lax.rem(q + i, n_q), z))

    relay(0)
    inverse = spd_inverse(gram)
    relay(1)
    solve(inverse, right)
    score(0)
    for i in range(2, n_t):
        relay(i)
        score(i - 1)
    ready(n_t - 1)
    load_rg.wait()
    others = x_all.at[pl.ds(0, (n_q - 1) * rank), :]
    landed(others, x_r)
    product = contract_last(x_all[...], rg_buf[...]) * (acc[...] + term(n_t - 1))
    totals = jnp.sum(product.reshape(n_q, rank, product.shape[1]), axis=1)
    out_ref[...] = totals * scale
    left(part_buf, rs_s)
    left(rs_buf, z_s)
    left(s_all.at[:, pl.ds(0, (n_q - 1) * rank), :], s_s)
    left(r_recv, f_s)
    left(others, x_s)


def local(query_acts, query_grads, sketch_maps, res_acts, res_grads):
    n_q, n_t = lax.axis_size("query"), lax.axis_size("tok")
    _, tokens, d_in = query_acts.shape
    d_out = query_grads.shape[2]
    rank = sketch_maps.shape[1]
    resident = res_acts.shape[0]
    width = d_in // n_t
    scale = 1.0 / math.sqrt(rank * d_out * tokens * n_t)
    n_chip = n_q // 2
    dma = pltpu.SemaphoreType.DMA
    vmem = pltpu.VMEM
    any_spec = pl.BlockSpec(memory_space=pl.ANY)
    return pl.pallas_call(
        functools.partial(kernel, n_q, n_t, scale),
        out_shape=pltpu.VMEM((n_q, resident), F32),
        in_specs=[any_spec] * 5,
        out_specs=pl.BlockSpec(memory_space=pltpu.VMEM),
        scratch_shapes=[
            vmem((n_t, tokens, width), BF16),
            vmem((tokens, d_out), BF16),
            vmem((rank, d_out), BF16),
            vmem((n_t, resident, width), BF16),
            vmem((resident, d_out), BF16),
            vmem((n_t - 1, rank, width), BF16),
            vmem((n_t - 1, rank, width), BF16),
            vmem((n_t, n_q * rank, width), BF16),
            vmem((rank, d_out), BF16),
            vmem((n_t - 1, rank, d_out), BF16),
            vmem((n_q * rank, d_out), BF16),
            vmem((n_q * rank, resident), F32),
            dma((n_t + 2,)),
            dma(()), dma((n_t - 1,)),
            dma(()), dma((n_t - 1,)),
            dma(()), dma((n_chip - 1, n_t)), dma((n_t,)),
            dma(()), dma(()),
            dma(()), dma(()),
        ],
        compiler_params=pltpu.CompilerParams(
            collective_id=0, has_side_effects=True, vmem_limit_bytes=60 * 1024 * 1024
        ),
    )(query_acts[0], query_grads[0], sketch_maps[0], res_acts, res_grads)


def solution(mesh):
    in_specs = (
        P("query", "tok", None),
        P("query", "tok", None),
        P("query", None, None),
        P(("query", "tok"), None),
        P(("query", "tok"), None),
    )
    out_specs = P(None, ("query", "tok"))
    return jax.shard_map(local, mesh=mesh, in_specs=in_specs, out_specs=out_specs, check_vma=False)
```

time: 30.3 us -> 29.4 us (0.970)
  Pallas kernels: 29.6 us -> 28.6 us
    pallas_call x1, Pallas kernels: 29.6 us -> 28.6 us  [local(): pl.pallas_call(functools.partial(kernel, n_q, n_t, scale), out_shape=pltp...]
where the time goes in v2:
time: 29.4 us; the launch traced here: 29.3 us
  Pallas kernels  28.6 us (97%)
  local copies, waits for them, and re-layouts  0.62 us (2%)
    pallas_call x1, Pallas kernels, local(): pl.pallas_call(functools.partial(kernel, n_q, n_t, scale), out_shape=pltp...  28.6 us
    unnamed x1, local copies, waits for them, and re-layouts  0.62 us

profile of v2, /device:TPU:0, one launch (start us, length us, event | category | flops | bytes accessed | tf_op | source)
XLA Modules:
  0.0 29.3 jit_solution(10210232028944039392)
XLA Ops:
  0.0 28.6 %shard_map.55 = f32[8,1024]{1,0:T(8,128)S(1)} custom-call(bf16[256,4096]{1,0:T(8,128)(2,1)} %bitcast.3, bf16[256,512]{1,0:T(8,128)(2,1)} %bitcast.4, bf16[32,512]{1,0:T(8,128)(2,1)} %bitcast.5, bf16[1024,4096]{1,0:T(8,128)(2,1)} %ra_hbm.1, bf16[1024,512]{1,0:T(8,128)(2,1)} %rg_hbm.1), custom_call_target="tpu_custom_call" | custom-call | tf_op jit(solution)/shard_map/pallas_call | solution.py:210
  28.6 0.6 %copy.7 = f32[8,1024]{1,0:T(8,128)} copy(f32[8,1024]{1,0:T(8,128)S(1)} %shard_map.55) | data formatting | bytes 65536

commit v3 on v2

--- a/solution.py
+++ b/solution.py
@@ -11,6 +11,7 @@
 MESH = pl.DeviceIdType.MESH
 F32 = jnp.float32
 BF16 = jnp.bfloat16
+HALVES = 2
 
 
 def contract_last(first_arr, second_arr):
@@ -42,12 +43,19 @@
     sibling = chip * 2 + 1 - core
     rank = m_buf.shape[0]
     width = a_buf.shape[2]
+    part_width = width // HALVES
 
     def tok_at(i):
         return lax.rem(z + i + n_t, n_t)
 
     def chip_at(c, which):
         return lax.rem(chip + c + n_chip, n_chip) * 2 + which
+
+    barrier = pltpu.get_barrier_semaphore()
+    for i in range(1, n_t):
+        pl.semaphore_signal(barrier, inc=1, device_id=(q, tok_at(i)), device_id_type=MESH)
+    for i in range(1, n_q):
+        pl.semaphore_signal(barrier, inc=1, device_id=(lax.rem(q + i, n_q), z), device_id_type=MESH)
 
     def load(src, dst, sem):
         copy = pltpu.make_async_copy(src, dst, local_sem.at[sem])
@@ -60,12 +68,6 @@
     for i in range(n_t):
         t = tok_at(i + 1)
         load_a.append(load(a_hbm.at[:, pl.ds(pl.multiple_of(t * width, width), width)], a_buf.at[t], 2 + i))
-    barrier = pltpu.get_barrier_semaphore()
-    for i in range(1, n_t):
-        pl.semaphore_signal(barrier, inc=1, device_id=(q, tok_at(i)), device_id_type=MESH)
-    for i in range(1, n_q):
-        pl.semaphore_signal(barrier, inc=1, device_id=(lax.rem(q + i, n_q), z), device_id_type=MESH)
-
     def remote(src, dst, send_sem, recv_sem, device):
         return pltpu.make_async_remote_copy(
             src_ref=src, dst_ref=dst, send_sem=send_sem, recv_sem=recv_sem, device_id=device, device_id_type=MESH
@@ -97,39 +99,58 @@
         load_ra.append(load(ra_hbm.at[:, pl.ds(pl.multiple_of(t * width, width), width)], ra_buf.at[t], 2 + i))
     load_rg = load(rg_hbm, rg_buf, 0)
     pl.semaphore_wait(barrier, n_t - 1 + n_q - 1)
+    def columns(h):
+        return pl.ds(h * part_width, part_width)
+
     for i in range(1, n_t):
-        send(part_buf.at[i - 1], rs_buf.at[i - 1], rs_s, rs_r.at[i - 1], (q, tok_at(i)))
-    for i in range(1, n_t):
-        landed(rs_buf.at[i - 1], rs_r.at[i - 1])
-        chunk = chunk + rs_buf[i - 1].astype(F32)
+        for h in range(HALVES):
+            there = rs_buf.at[i - 1, :, columns(h)]
+            send(part_buf.at[i - 1, :, columns(h)], there, rs_s, rs_r.at[i - 1, h], (q, tok_at(i)))
 
     def block(t, owner):
         return s_all.at[t, pl.ds(pl.multiple_of(owner * rank, rank), rank), :]
 
-    s_all[z, pl.ds(pl.multiple_of(q * rank, rank), rank), :] = chunk.astype(BF16)
+    def half_block(t, h):
+        return s_all.at[t, pl.ds(pl.multiple_of(q * rank, rank), rank), columns(h)]
 
     def from_chip(c, i):
         return c_r.at[c - 1, i]
 
-    def spread(i):
-        here = block(tok_at(-i), q)
+    def spread(i, h):
+        here = half_block(tok_at(-i), h)
         for c in range(1, n_chip):
             send(here, here, s_s, from_chip(c, i), (chip_at(c, core), z))
         send(here, here, s_s, b_r.at[i], (sibling, z))
 
-    for i in range(1, n_t):
-        send(block(z, q), block(z, q), z_s, z_r.at[i - 1], (q, tok_at(i)))
-    gram = jnp.zeros((rank, rank), F32)
+    def pull(i, h):
+        t = tok_at(-i)
+        return contract_last(half_block(t, h)[...], a_buf[t, :, columns(h)])
+
+    def square(i):
+        mine = s_all[tok_at(-i), pl.ds(pl.multiple_of(q * rank, rank), rank), :]
+        return contract_last(mine, mine)
+
     pulled = jnp.zeros((rank, g_buf.shape[0]), F32)
-    for i in range(n_t):
-        t = tok_at(-i)
-        if i:
-            landed(block(t, q), z_r.at[i - 1])
-        spread(i)
-        mine = s_all[t, pl.ds(pl.multiple_of(q * rank, rank), rank), :]
-        pulled += contract_last(mine, a_buf[t])
-        if i < n_t - 1:
-            gram += contract_last(mine, mine)
+    for h in range(HALVES):
+        total = chunk[:, h * part_width : (h + 1) * part_width]
+        for i in range(1, n_t):
+            there = rs_buf.at[i - 1, :, columns(h)]
+            landed(there, rs_r.at[i - 1, h])
+            total = total + there[...].astype(F32)
+        here = half_block(z, h)
+        here[...] = total.astype(BF16)
+        for i in range(1, n_t):
+            send(here, here, z_s, z_r.at[i - 1, h], (q, tok_at(i)))
+        spread(0, h)
+        pulled += pull(0, h)
+    gram = square(0)
+    for h in range(HALVES):
+        for i in range(1, n_t):
+            landed(half_block(tok_at(-i), h), z_r.at[i - 1, h])
+            spread(i, h)
+            pulled += pull(i, h)
+            if h == HALVES - 1 and i < n_t - 1:
+                gram += square(i)
     high = pulled.astype(BF16)
     low = (pulled - high.astype(F32)).astype(BF16)
     grads = g_buf[...]
@@ -137,7 +158,7 @@
     r_mine[...] = right.astype(BF16)
     for i in range(1, n_t):
         send(r_mine, r_recv.at[i - 1], f_s, f_r, (q, tok_at(i)))
-    gram += contract_last(mine, mine)
+    gram += square(n_t - 1)
 
     def relay(i):
         t = tok_at(-i)
@@ -175,17 +196,19 @@
 
     relay(0)
     inverse = spd_inverse(gram)
+    solve(inverse, right)
     relay(1)
-    solve(inverse, right)
     score(0)
     for i in range(2, n_t):
         relay(i)
         score(i - 1)
     ready(n_t - 1)
+    last = tok_at(1 - n_t)
+    acc[...] += contract_last(s_all[last, :, columns(0)], ra_buf[last, :, columns(0)])
     load_rg.wait()
     others = x_all.at[pl.ds(0, (n_q - 1) * rank), :]
     landed(others, x_r)
-    product = contract_last(x_all[...], rg_buf[...]) * (acc[...] + term(n_t - 1))
+    product = contract_last(x_all[...], rg_buf[...]) * (acc[...] + contract_last(s_all[last, :, columns(1)], ra_buf[last, :, columns(1)]))
     totals = jnp.sum(product.reshape(n_q, rank, product.shape[1]), axis=1)
     out_ref[...] = totals * scale
     left(part_buf, rs_s)
@@ -226,8 +249,8 @@
             vmem((n_q * rank, d_out), BF16),
             vmem((n_q * rank, resident), F32),
             dma((n_t + 2,)),
-            dma(()), dma((n_t - 1,)),
-            dma(()), dma((n_t - 1,)),
+            dma(()), dma((n_t - 1, HALVES)),
+            dma(()), dma((n_t - 1, HALVES)),
             dma(()), dma((n_chip - 1, n_t)), dma((n_t,)),
             dma(()), dma(()),
             dma(()), dma(()),

time: 29.4 us -> 29.1 us (0.990)
  Pallas kernels: 28.6 us -> 28.3 us
where the time goes in v3:
time: 29.1 us; the launch traced here: 29 us
  Pallas kernels  28.3 us (97%)
  local copies, waits for them, and re-layouts  0.62 us (2%)
    pallas_call x1, Pallas kernels, local(): pl.pallas_call(functools.partial(kernel, n_q, n_t, scale), out_shape=pltp...  28.3 us
    unnamed x1, local copies, waits for them, and re-layouts  0.62 us

profile of v3, /device:TPU:0, one launch (start us, length us, event | category | flops | bytes accessed | tf_op | source)
XLA Modules:
  0.0 29.0 jit_solution(10272817404815294115)
XLA Ops:
  0.0 28.3 %shard_map.55 = f32[8,1024]{1,0:T(8,128)S(1)} custom-call(bf16[256,4096]{1,0:T(8,128)(2,1)} %bitcast.3, bf16[256,512]{1,0:T(8,128)(2,1)} %bitcast.4, bf16[32,512]{1,0:T(8,128)(2,1)} %bitcast.5, bf16[1024,4096]{1,0:T(8,128)(2,1)} %ra_hbm.1, bf16[1024,512]{1,0:T(8,128)(2,1)} %rg_hbm.1), custom_call_target="tpu_custom_call" | custom-call | tf_op jit(solution)/shard_map/pallas_call | solution.py:233
  28.3 0.6 %copy.7 = f32[8,1024]{1,0:T(8,128)} copy(f32[8,1024]{1,0:T(8,128)S(1)} %shard_map.55) | data formatting | bytes 65536

commit v4 on v3

--- a/solution.py
+++ b/solution.py
@@ -35,7 +35,7 @@
     a_hbm, g_hbm, m_hbm, ra_hbm, rg_hbm, out_ref,
     a_buf, g_buf, m_buf, ra_buf, rg_buf,
     part_buf, rs_buf, s_all, r_mine, r_recv, x_all, acc,
-    local_sem, rs_s, rs_r, z_s, z_r, s_s, c_r, b_r, f_s, f_r, x_s, x_r,
+    local_sem, rs_s, rs_r, z_s, z_r, s_s, c_r, c_last, b_r, f_s, f_r, x_s, x_r,
 ):
     q, z = lax.axis_index("query"), lax.axis_index("tok")
     n_chip = n_q // 2
@@ -110,17 +110,20 @@
     def block(t, owner):
         return s_all.at[t, pl.ds(pl.multiple_of(owner * rank, rank), rank), :]
 
-    def half_block(t, h):
-        return s_all.at[t, pl.ds(pl.multiple_of(q * rank, rank), rank), columns(h)]
-
-    def from_chip(c, i):
-        return c_r.at[c - 1, i]
+    def half_block(t, h, owner=q):
+        return s_all.at[t, pl.ds(pl.multiple_of(owner * rank, rank), rank), columns(h)]
+
+    def from_chip(c, i, h):
+        return c_last.at[c - 1] if (i, h) == (n_t - 1, HALVES - 1) else c_r.at[i, h if i else 0]
+
+    def from_core(i, h):
+        return b_r.at[i, h if i else 0]
 
     def spread(i, h):
         here = half_block(tok_at(-i), h)
         for c in range(1, n_chip):
-            send(here, here, s_s, from_chip(c, i), (chip_at(c, core), z))
-        send(here, here, s_s, b_r.at[i], (sibling, z))
+            send(here, here, s_s, from_chip(c, i, h), (chip_at(c, core), z))
+        send(here, here, s_s, from_core(i, h), (sibling, z))
 
     def pull(i, h):
         t = tok_at(-i)
@@ -160,27 +163,37 @@
         send(r_mine, r_recv.at[i - 1], f_s, f_r, (q, tok_at(i)))
     gram += square(n_t - 1)
 
-    def relay(i):
+    def first(n, i, h):
+        there = s_all.at[tok_at(-i), pl.ds(0, n * rank)]
+        return there.at[:, columns(h)] if i else there
+
+    def relay(i, h):
+        t, chipwise = tok_at(-i), (i, h) == (n_t - 1, HALVES - 1)
+        if not chipwise:
+            landed(first(n_chip - 1, i, h), from_chip(1, i, h))
+        for c in range(1, n_chip):
+            owner = chip_at(-c, core)
+            here = half_block(t, h, owner) if i else block(t, owner)
+            if chipwise:
+                landed(here, from_chip(c, i, h))
+            send(here, here, s_s, from_core(i, h), (sibling, z))
+
+    def ready(i, h):
+        landed(first(n_chip, i, h), from_core(i, h))
+        if h == 0:
+            load_ra[i].wait()
+
+    def term(i, h):
         t = tok_at(-i)
-        for c in range(1, n_chip):
-            here = block(t, chip_at(-c, core))
-            landed(here, from_chip(c, i))
-            send(here, here, s_s, b_r.at[i], (sibling, z))
-
-    def ready(i):
-        landed(s_all.at[tok_at(-i), pl.ds(0, n_chip * rank)], b_r.at[i])
-        load_ra[i].wait()
-
-    def term(i):
-        t = tok_at(-i)
-        return contract_last(s_all[t], ra_buf[t])
-
-    def score(i):
-        ready(i)
-        if i == 0:
-            acc[...] = term(i)
-        else:
-            acc[...] += term(i)
+        return contract_last(s_all[t, :, columns(h)], ra_buf[t, :, columns(h)])
+
+    def score(places, h):
+        for i in places:
+            ready(i, h)
+        total = acc[...]
+        for i in places:
+            total = total + term(i, h)
+        acc[...] = total
 
     def x_block(owner):
         return x_all.at[pl.ds(pl.multiple_of(owner * rank, rank), rank), :]
@@ -194,21 +207,27 @@
         for i in (*range(2, n_q), 1):
             send(x_block(q), x_block(q), x_s, x_r, (lax.rem(q + i, n_q), z))
 
-    relay(0)
+    rest, final = range(1, n_t), HALVES - 1
+    relay(0, 0)
     inverse = spd_inverse(gram)
+    for i in rest[:-1]:
+        relay(i, 0)
     solve(inverse, right)
-    relay(1)
-    score(0)
-    for i in range(2, n_t):
-        relay(i)
-        score(i - 1)
-    ready(n_t - 1)
-    last = tok_at(1 - n_t)
-    acc[...] += contract_last(s_all[last, :, columns(0)], ra_buf[last, :, columns(0)])
+    relay(n_t - 1, 0)
+    ready(0, 0)
+    acc[...] = contract_last(s_all[z], ra_buf[z])
+    relay(1, final)
+    score(rest, 0)
+    for i in rest[1:-1]:
+        relay(i, final)
+    score(rest[:1], final)
+    relay(n_t - 1, final)
+    score(rest[1:-1], final)
+    ready(n_t - 1, final)
     load_rg.wait()
     others = x_all.at[pl.ds(0, (n_q - 1) * rank), :]
     landed(others, x_r)
-    product = contract_last(x_all[...], rg_buf[...]) * (acc[...] + contract_last(s_all[last, :, columns(1)], ra_buf[last, :, columns(1)]))
+    product = contract_last(x_all[...], rg_buf[...]) * (acc[...] + term(n_t - 1, final))
     totals = jnp.sum(product.reshape(n_q, rank, product.shape[1]), axis=1)
     out_ref[...] = totals * scale
     left(part_buf, rs_s)
@@ -251,7 +270,7 @@
             dma((n_t + 2,)),
             dma(()), dma((n_t - 1, HALVES)),
             dma(()), dma((n_t - 1, HALVES)),
-            dma(()), dma((n_chip - 1, n_t)), dma((n_t,)),
+            dma(()), dma((n_t, HALVES)), dma((n_chip - 1,)), dma((n_t, HALVES)),
             dma(()), dma(()),
             dma(()), dma(()),
         ],

time: 29.1 us -> 29 us (level)
  no operation moved by 1% of the time
where the time goes in v4:
time: 29 us; the launch traced here: 28.8 us
  Pallas kernels  28.2 us (97%)
  local copies, waits for them, and re-layouts  0.62 us (2%)
    pallas_call x1, Pallas kernels, local(): pl.pallas_call(functools.partial(kernel, n_q, n_t, scale), out_shape=pltp...  28.2 us
    unnamed x1, local copies, waits for them, and re-layouts  0.62 us

profile of v4, /device:TPU:0, one launch (start us, length us, event | category | flops | bytes accessed | tf_op | source)
XLA Modules:
  0.0 28.8 jit_solution(12068750850382276226)
XLA Ops:
  0.0 28.2 %shard_map.55 = f32[8,1024]{1,0:T(8,128)S(1)} custom-call(bf16[256,4096]{1,0:T(8,128)(2,1)} %bitcast.3, bf16[256,512]{1,0:T(8,128)(2,1)} %bitcast.4, bf16[32,512]{1,0:T(8,128)(2,1)} %bitcast.5, bf16[1024,4096]{1,0:T(8,128)(2,1)} %ra_hbm.1, bf16[1024,512]{1,0:T(8,128)(2,1)} %rg_hbm.1), custom_call_target="tpu_custom_call" | custom-call | tf_op jit(solution)/shard_map/pallas_call | solution.py:252
  28.2 0.6 %copy.7 = f32[8,1024]{1,0:T(8,128)} copy(f32[8,1024]{1,0:T(8,128)S(1)} %shard_map.55) | data formatting | bytes 65536

commit v5 on v4

--- a/solution.py
+++ b/solution.py
@@ -113,11 +113,14 @@
     def half_block(t, h, owner=q):
         return s_all.at[t, pl.ds(pl.multiple_of(owner * rank, rank), rank), columns(h)]
 
+    def slot(i, h):
+        return (i - 1) * HALVES + h + 1 if i else 0
+
     def from_chip(c, i, h):
-        return c_last.at[c - 1] if (i, h) == (n_t - 1, HALVES - 1) else c_r.at[i, h if i else 0]
+        return c_last.at[c - 1] if (i, h) == (n_t - 1, HALVES - 1) else c_r.at[slot(i, h)]
 
     def from_core(i, h):
-        return b_r.at[i, h if i else 0]
+        return b_r.at[slot(i, h)]
 
     def spread(i, h):
         here = half_block(tok_at(-i), h)
@@ -270,7 +273,7 @@
             dma((n_t + 2,)),
             dma(()), dma((n_t - 1, HALVES)),
             dma(()), dma((n_t - 1, HALVES)),
-            dma(()), dma((n_t, HALVES)), dma((n_chip - 1,)), dma((n_t, HALVES)),
+            dma(()), dma(((n_t - 1) * HALVES,)), dma((n_chip - 1,)), dma(((n_t - 1) * HALVES + 1,)),
             dma(()), dma(()),
             dma(()), dma(()),
         ],

time: 29 us -> 28.9 us (level)
  no operation moved by 1% of the time
where the time goes in v5:
time: 28.9 us; the launch traced here: 28.8 us
  Pallas kernels  28.2 us (98%)
  local copies, waits for them, and re-layouts  0.62 us (2%)
    pallas_call x1, Pallas kernels, local(): pl.pallas_call(functools.partial(kernel, n_q, n_t, scale), out_shape=pltp...  28.2 us
    unnamed x1, local copies, waits for them, and re-layouts  0.62 us

profile of v5, /device:TPU:0, one launch (start us, length us, event | category | flops | bytes accessed | tf_op | source)
XLA Modules:
  0.0 28.8 jit_solution(7517957427153192149)
XLA Ops:
  0.0 28.2 %shard_map.55 = f32[8,1024]{1,0:T(8,128)S(1)} custom-call(bf16[256,4096]{1,0:T(8,128)(2,1)} %bitcast.3, bf16[256,512]{1,0:T(8,128)(2,1)} %bitcast.4, bf16[32,512]{1,0:T(8,128)(2,1)} %bitcast.5, bf16[1024,4096]{1,0:T(8,128)(2,1)} %ra_hbm.1, bf16[1024,512]{1,0:T(8,128)(2,1)} %rg_hbm.1), custom_call_target="tpu_custom_call" | custom-call | tf_op jit(solution)/shard_map/pallas_call | solution.py:255
  28.2 0.6 %copy.7 = f32[8,1024]{1,0:T(8,128)} copy(f32[8,1024]{1,0:T(8,128)S(1)} %shard_map.55) | data formatting | bytes 65536
